TPU v7x, 32 devices: a whole 2x2x4 slice. The times are simulated.
32 devices in a mesh: ctx: 16 (over z, x, core), head: 2 (over y).
Axes of the slice: x: 2, y: 2, z: 4, core: 2. Of those that a mesh axis runs over, the one named last changes fastest.
Arguments:
- query_rows: bfloat16 [8192, 2048], P('ctx', 'head'), may hold values from -60 to 60
- key_rows: bfloat16 [8192, 2048], P('ctx', 'head'), may hold values from -6 to 6
- value_rows: bfloat16 [8192, 2048], P('ctx', 'head'), may hold values from -60 to 60
- log_gate: float32 [16, 8192], P('head', 'ctx'), may hold values from -0.5 to 0
- conv_weight: float32 [3, 4, 2048], P(None, None, 'head'), may hold values from -3 to 3
- norm_gain: float32 [2048], P('head'), may hold values from 0.5 to 1.5
- mixed_grad: bfloat16 [8192, 2048], P('ctx', 'head'), may hold values from -24 to 24
Outputs:
- mixer_out: bfloat16 [8192, 2048], P('ctx', 'head')
- query_grad: bfloat16 [8192, 2048], P('ctx', 'head')
- key_grad: bfloat16 [8192, 2048], P('ctx', 'head')
- value_grad: bfloat16 [8192, 2048], P('ctx', 'head')
- conv_grad: float32 [3, 4, 2048], P(None, None, 'head')
- gain_grad: float32 [2048], P('head')
All inputs are finite; a program needn't handle non-finite values.
Results may differ from a plain program's by a relative error of at most 0.015.
Values may be sent and summed in bfloat16 or wider, within the bound.
A program may use at most 128 MiB of HBM per device.

v0:
```python
import jax
import jax.numpy as jnp
from jax import lax
from jax.sharding import PartitionSpec as P

HD = 128
TAPS = 4
GROUP = 512
D = 2048


norm_epsilon = 1e-05


def shifted(block, axis, distance):
    devices = range(lax.axis_size(axis))
    route = [(i - distance, i) for i in devices if i - distance in devices]
    return lax.ppermute(block, axis, route)


def prefix(value, axis, join, neutral):
    count = lax.axis_size(axis)
    place = lax.axis_index(axis)
    ahead = count - 1 - place
    gathered = jax.tree.map(
        lambda a, kind: lax.all_gather(a.astype(kind), axis), value, (jnp.bfloat16, jnp.bfloat16)
    )
    state = jax.tree.map(lambda a, e: jnp.zeros_like(a) + jnp.asarray(e, a.dtype), value, neutral)

    def one(turn, state):
        source = count - 1 - turn
        return join(
            state,
            jax.tree.map(
                lambda a, own: lax.dynamic_index_in_dim(a, source, 0, False).astype(own.dtype),
                gathered,
                value,
            ),
        )

    return lax.fori_loop(0, ahead, one, state)


def rounded(values):
    return values.astype(jnp.bfloat16)


def decay_tables(gate_blocks):
    running = jnp.cumsum(gate_blocks, axis=-1)
    closing = running[..., -1]
    gap_matrix = running[..., :, None] - running[..., None, :]
    block_size = gate_blocks.shape[-1]
    lower_mask = jnp.arange(block_size)[:, None] >= jnp.arange(block_size)[None, :]
    weights = jnp.where(lower_mask, jnp.exp(jnp.minimum(gap_matrix, 0.0)), 0.0)
    return (running, closing, weights)


def chain_step(earlier, later_part):
    return (
        earlier[0] + later_part[0],
        jnp.exp(later_part[0])[..., None, None] * earlier[1] + later_part[1],
    )


def local_chain(closing, blocks, backwards):

    def advance(partial_sum, block_item):
        return (chain_step(partial_sum, block_item), partial_sum)

    initial = (jnp.zeros(closing.shape[1:], jnp.float32), jnp.zeros(blocks.shape[1:], jnp.float32))
    return lax.scan(advance, initial, (closing, blocks), reverse=backwards)


def conv_forward(rim_rows, rows, weight, tok_here):
    extended = jnp.concatenate([rim_rows, rows], axis=0).astype(jnp.float32)
    result = weight[0][None, :] * extended[TAPS - 1 : TAPS - 1 + tok_here]
    for offset in range(1, TAPS):
        result = (
            result
            + weight[offset][None, :] * extended[TAPS - 1 - offset : TAPS - 1 - offset + tok_here]
        )
    return (rounded(result), extended)


def conv_backward(grad_rows, edge_rows, extended, weight, tok_here):
    ahead_all = jnp.concatenate([grad_rows, edge_rows], axis=0)
    input_grad = weight[0][None, :] * grad_rows
    weight_grad = [jnp.sum(grad_rows * extended[TAPS - 1 : TAPS - 1 + tok_here], axis=0)]
    for offset in range(1, TAPS):
        input_grad = input_grad + weight[offset][None, :] * ahead_all[offset : offset + tok_here]
        weight_grad.append(
            jnp.sum(grad_rows * extended[TAPS - 1 - offset : TAPS - 1 - offset + tok_here], axis=0)
        )
    return (rounded(input_grad), jnp.stack(weight_grad))


def body(query_rows, key_rows, value_rows, log_gate, conv_weight, norm_gain, mixed_grad):
    tok_here = query_rows.shape[0]
    width_here = query_rows.shape[1]
    heads_here = width_here // HD
    block_count = tok_here // GROUP
    rim_rows = shifted(
        jnp.stack(
            [
                query_rows[tok_here - (TAPS - 1) :],
                key_rows[tok_here - (TAPS - 1) :],
                value_rows[tok_here - (TAPS - 1) :],
            ]
        ),
        "ctx",
        1,
    )
    query_conv, query_ext = conv_forward(rim_rows[0], query_rows, conv_weight[0], tok_here)
    key_conv, key_ext = conv_forward(rim_rows[1], key_rows, conv_weight[1], tok_here)
    value_conv, value_ext = conv_forward(rim_rows[2], value_rows, conv_weight[2], tok_here)
    query_blocks = query_conv.reshape(block_count, GROUP, heads_here, HD)
    key_blocks = key_conv.reshape(block_count, GROUP, heads_here, HD)
    value_blocks = value_conv.reshape(block_count, GROUP, heads_here, HD)
    gate_blocks = log_gate.reshape(heads_here, block_count, GROUP).transpose(1, 0, 2)
    running, closing, weights = decay_tables(gate_blocks)
    grow_factor = jnp.exp(running).transpose(0, 2, 1)[..., None]
    shrink = jnp.exp(closing[..., None] - running).transpose(0, 2, 1)[..., None]
    scores = jnp.einsum(
        "nthd,nshd->nhts", query_blocks, key_blocks, preferred_element_type=jnp.float32
    )
    weights_low = rounded(scores * weights)
    key_scaled = rounded(key_blocks * shrink)
    blocks = jnp.einsum(
        "nshd,nshe->nhde", key_scaled, value_blocks, preferred_element_type=jnp.float32
    )
    device_sum, before = local_chain(closing, blocks, False)
    zero_state = jnp.zeros((heads_here, HD, HD), jnp.float32)
    all_totals = lax.all_gather(device_sum[0][None], "ctx", axis=0, tiled=True)
    device_index = lax.axis_index("ctx")
    cumulative = jnp.cumsum(all_totals, axis=0)
    before_me = cumulative[device_index] - all_totals[device_index]
    sources = jnp.arange(all_totals.shape[0])
    factor_table = jnp.where(
        (sources < device_index)[:, None],
        jnp.exp(jnp.minimum(before_me[None, :] - cumulative, 0.0)),
        0.0,
    )
    incoming = jnp.einsum(
        "nh,nhde->hde",
        factor_table,
        lax.all_gather(device_sum[1][None], "ctx", axis=0, tiled=True),
        precision=lax.Precision.HIGHEST,
    )
    group_in = jnp.exp(before[0])[..., None, None] * incoming[None] + before[1]
    state_low = rounded(group_in)
    attended = jnp.einsum(
        "nhts,nshe->nthe", weights_low, value_blocks, preferred_element_type=jnp.float32
    )
    attended = (
        attended
        + jnp.einsum("nthd,nhde->nthe", query_blocks, state_low, preferred_element_type=jnp.float32)
        * grow_factor
    )
    attended = attended.reshape(tok_here, width_here)
    grad_wide = mixed_grad.astype(jnp.float32)
    scaled = grad_wide * norm_gain[None, :]
    squares = lax.psum(jnp.sum(attended * attended, axis=1), "head")
    inverse = lax.rsqrt(squares / D + norm_epsilon)
    inner_sum = lax.psum(jnp.sum(scaled * attended, axis=1), "head") / D
    normed = attended * inverse[:, None]
    mixer_out = rounded(normed * norm_gain[None, :])
    gain_part = jnp.sum(grad_wide * normed, axis=0)
    out_grad = rounded(
        inverse[:, None] * (scaled - attended * (inverse * inverse * inner_sum)[:, None])
    )
    grad_blocks = out_grad.reshape(block_count, GROUP, heads_here, HD)
    grad_scores = rounded(
        jnp.einsum("nthe,nshe->nhts", grad_blocks, value_blocks, preferred_element_type=jnp.float32)
        * weights
    )
    query_scaled = rounded(query_blocks * grow_factor)
    back_blocks = jnp.einsum(
        "nthd,nthe->nhde", query_scaled, grad_blocks, preferred_element_type=jnp.float32
    )
    back_sum, back_before = local_chain(closing, back_blocks, True)
    later_state = prefix(
        (back_sum[0], back_sum[1]),
        "ctx",
        chain_step,
        (jnp.zeros((heads_here,), jnp.float32), zero_state),
    )[1]
    later_low = rounded(
        jnp.exp(back_before[0])[..., None, None] * later_state[None] + back_before[1]
    )
    query_cg = jnp.einsum(
        "nhts,nshd->nthd", grad_scores, key_blocks, preferred_element_type=jnp.float32
    )
    query_cg = (
        query_cg
        + jnp.einsum("nthe,nhde->nthd", grad_blocks, state_low, preferred_element_type=jnp.float32)
        * grow_factor
    )
    key_cg = jnp.einsum(
        "nhts,nthd->nshd", grad_scores, query_blocks, preferred_element_type=jnp.float32
    )
    key_cg = (
        key_cg
        + jnp.einsum("nshe,nhde->nshd", value_blocks, later_low, preferred_element_type=jnp.float32)
        * shrink
    )
    value_cg = jnp.einsum(
        "nhts,nthe->nshe", weights_low, grad_blocks, preferred_element_type=jnp.float32
    )
    value_cg = (
        value_cg
        + jnp.einsum("nshd,nhde->nshe", key_blocks, later_low, preferred_element_type=jnp.float32)
        * shrink
    )
    query_cg = query_cg.reshape(tok_here, width_here)
    key_cg = key_cg.reshape(tok_here, width_here)
    value_cg = value_cg.reshape(tok_here, width_here)
    edge_rows = shifted(
        jnp.stack([query_cg[: TAPS - 1], key_cg[: TAPS - 1], value_cg[: TAPS - 1]]), "ctx", -1
    )
    query_grad, query_taps = conv_backward(
        query_cg, edge_rows[0], query_ext, conv_weight[0], tok_here
    )
    key_grad, key_taps = conv_backward(key_cg, edge_rows[1], key_ext, conv_weight[1], tok_here)
    value_grad, value_taps = conv_backward(
        value_cg, edge_rows[2], value_ext, conv_weight[2], tok_here
    )
    conv_part = jnp.stack([query_taps, key_taps, value_taps])
    conv_grad, gain_grad = lax.psum((conv_part, gain_part), "ctx")
    return (mixer_out, query_grad, key_grad, value_grad, conv_grad, gain_grad)


def solution(mesh):
    placed = (
        P("ctx", "head"),
        P("ctx", "head"),
        P("ctx", "head"),
        P("head", "ctx"),
        P(None, None, "head"),
        P("head"),
        P("ctx", "head"),
    )
    return jax.shard_map(
        body,
        mesh=mesh,
        in_specs=placed,
        out_specs=(
            P("ctx", "head"),
            P("ctx", "head"),
            P("ctx", "head"),
            P("ctx", "head"),
            P(None, None, "head"),
            P("head"),
        ),
        check_vma=False,
    )
```

profile of v0, /device:TPU:0, one launch (start us, length us, event | category | flops | bytes accessed | tf_op | source)
XLA Modules:
  0.0 309.8 jit_solution(4000271757423066720)
XLA Ops:
  8.8 2.4 collective-permute-start
  11.2 2.2 reduce-window.6
  13.7 1.0 fusion.61
  16.5 1.7 maximum_convert_fusion
  18.5 1.0 fusion.79
  19.7 1.5 copy.163
  21.2 4.9 %fusion.49 = bf16[64,8,8,128]{3,2,1,0:T(8,128)(2,1)S(1)} fusion(f32[515,1024]{1,0:T(8,128)} %maximum_convert_fusion, f32[1024]{0:T(1024)S(1)} %bitcast.226, f32[1024]{0:T(1024)S(1)} %bitcast.228, f32[1024]{0:T(1024)S(1)} %bitcast.230, f32[1024]{0:T(1024)S(1)} %bitcast.224), kind=kLoop, calls=%fused_computation.94 | loop fusion | flops 4194304 | bytes 9453568
  26.1 1.3 convolution_add_fusion.1
  27.5 1.0 copy.168
  28.5 22.8 %all-gather = f32[16,8,1]{1,2,0:T(1,128)S(1)} all-gather(f32[1,8,1]{1,2,0:T(1,128)S(1)} %get-tuple-element.187), channel_id=2, replica_groups=mesh['ctx'=16,'head'=2] {'ctx'}, dimensions={0}, use_global_device_ids=true | all-gather | bytes 544 | tf_op jit(solution)/shard_map/all_gather | solution.py:133
  52.4 1.4 bitcast_add_fusion
  53.7 1.5 maximum_convert_fusion.1
  55.3 1.3 copy-done
  56.6 1.9 add_convert_fusion.1
  58.5 2.3 copy.213
  62.0 2.9 multiply_convert_fusion.1
  65.0 2.0 copy-done.2
  66.9 2.8 fusion.42
  69.8 35.3 %all-gather.7.cloned.1.call-done = f32[128,128,128]{2,1,0:T(8,128)} async-done(((f32[8,128,128]{2,1,0:T(8,128)}), f32[128,128,128]{2,1,0:T(8,128)}) %all-gather.7.cloned.1.call-update) | async-done | bytes 8388624 | tf_op jit(solution)/shard_map/all_gather | solution.py:146
  105.1 12.5 %fusion = f32[8,1,128,128]{3,1,2,0:T(1,128)S(1)} fusion(f32[16,8,1,1]{0,2,3,1:T(1,128)S(1)} %copy.206, f32[16,8,128,128]{3,2,1,0:T(8,128)} %bitcast.188), kind=kOutput, calls=%fused_computation.2 | convolution fusion | flops 25165824 | bytes 8913408 | tf_op jit(solution)/shard_map/nh,nhde->hde/dot_general | solution.py:143
  117.6 1.9 multiply_reduce_fusion.12
  119.5 5.1 %psum.28 = f32[512]{0:T(512)S(1)} all-reduce(f32[512]{0:T(512)S(1)} %get-tuple-element.206), channel_id=1, replica_groups=mesh['ctx'=16,'head'=2] {'head'}, use_global_device_ids=true, to_apply=%region_4.5 | all-reduce | flops 512 | bytes 4096 | tf_op jit(solution)/shard_map/psum | solution.py:162
  124.7 2.9 copy.169
  127.6 2.6 fusion.7
  130.2 4.9 %psum.29 = f32[512]{0:T(512)S(1)} all-reduce(f32[512]{0:T(512)S(1)} %get-tuple-element.166), channel_id=1, replica_groups=mesh['ctx'=16,'head'=2] {'head'}, use_global_device_ids=true, to_apply=%region_6.7 | all-reduce | flops 512 | bytes 4096 | tf_op jit(solution)/shard_map/psum | solution.py:164
  135.2 3.9 %fusion.6 = (bf16[512,1024]{1,0:T(8,128)(2,1)}, bf16[512,1024]{1,0:T(8,128)(2,1)}) fusion(bf16[512,1024]{1,0:T(8,128)(2,1)} %param.15, f32[512,1024]{1,0:T(8,128)} %copy.169, f32[512]{0:T(512)S(1)} %multiply_multiply_fusion, f32[1024]{0:T(1024)S(1)} %copy-done.25, f32[512]{0:T(512)S(1)} %add_rsqrt_fusion), kind=kLoop, calls=%fused_computation.19 | loop fusion | flops 4718592 | bytes 5251072 | tf_op jit(solution)/shard_map/convert_element_type | solution.py:45
  139.0 2.3 copy.214
  141.3 2.7 fusion.39
  144.0 18.6 %all-gather.3 = bf16[16,8,1]{1,2,0:T(2,128)(2,1)S(1)} all-gather(bf16[1,8,1]{1,2,0:T(2,128)(2,1)S(1)} %slice.396), channel_id=5, replica_groups=mesh['ctx'=16,'head'=2] {'ctx'}, dimensions={0}, use_global_device_ids=true | all-gather | bytes 272 | tf_op jit(solution)/shard_map/all_gather | solution.py:26
  162.7 4.0 %multiply_convert_fusion = bf16[8,512,512]{2,1,0:T(8,128)(2,1)S(1)} fusion(f32[8,512]{1,0:T(8,128)S(1)} %copy-done.27, pred[512,512]{1,0:T(8,128)(4,1)} %iota_compare_fusion, bf16[512,8,128]{0,2,1:T(8,128)(2,1)} %bitcast.185, bf16[64,8,8,128]{3,2,1,0:T(8,128)(2,1)S(1)} %fusion.49), kind=kOutput, calls=%fused_computation.4 | convolution fusion | flops 547356672 | bytes 6569984 | tf_op jit(solution)/shard_map/nthe,nshe->nhts/dot_general | solution.py:173
  166.7 1.5 fusion.62
  169.7 1.3 copy-done.5
  171.9 1.2 copy.186
  173.1 4.4 %fusion.64 = f32[8,128,512]{2,1,0:T(8,128)} fusion(bf16[512,8,128]{0,2,1:T(8,128)(2,1)S(1)} %bitcast.187, bf16[8,512,512]{2,1,0:T(8,128)(2,1)} %copy-done.2), kind=kOutput, calls=%fused_computation.139 | convolution fusion | flops 536870912 | bytes 7340032 | tf_op jit(solution)/shard_map/nhts,nthe->nshe/dot_general | solution.py:206
  177.5 2.0 fusion.63
  179.6 13.5 %all-gather.9.cloned.1.call-done = bf16[128,128,128]{2,1,0:T(8,128)(2,1)} async-done(((bf16[8,128,128]{2,1,0:T(8,128)(2,1)}), bf16[128,128,128]{2,1,0:T(8,128)(2,1)}) %all-gather.9.cloned.1.call-update) | async-done | bytes 4194320 | tf_op jit(solution)/shard_map/all_gather | solution.py:26
  193.1 17.3 %while.9 = (s32[]{:T(128)}, f32[8,128,128]{2,1,0:T(8,128)S(1)}, s32[]{:T(128)}, bf16[16,8]{1,0:T(8,128)(2,1)S(1)}, bf16[16,8,128,128]{3,2,1,0:T(8,128)(2,1)}, /*index=5*/s32[]{:T(128)}, s32[]{:T(128)}, s32[]{:T(128)}, s32[]{:T(128)}) while((s32[]{:T(128)}, f32[8,128,128]{2,1,0:T(8,128)S(1)}, s32[]{:T(128)}, bf16[16,8]{1,0:T(8,128)(2,1)S(1)}, ...), condition=%wide.region_8.9_spmd, body=%wide.region_7.8_spmd.sunk | while | flops 393230 | bytes 1310955 | solution.py:41
  193.2 1.1 convert_add_fusion.2
  194.3 1.1 convert_add_fusion.2
  195.5 1.1 convert_add_fusion.2
  196.6 1.1 convert_add_fusion.2
  197.8 1.1 convert_add_fusion.2
  198.9 1.1 convert_add_fusion.2
  200.1 1.1 convert_add_fusion.2
  201.2 1.1 convert_add_fusion.2
  202.4 1.1 convert_add_fusion.2
  203.6 1.1 convert_add_fusion.2
  204.7 1.1 convert_add_fusion.2
  205.9 1.1 convert_add_fusion.2
  207.0 1.1 convert_add_fusion.2
  208.2 1.1 convert_add_fusion.2
  209.3 1.1 convert_add_fusion.2
  210.4 2.4 fusion.35
  212.9 1.3 copy-done.6
  214.4 2.4 fusion.36
  216.8 1.3 copy-done.7
  218.4 1.6 collective-permute-start.1
  220.0 3.0 copy.176
  222.9 2.9 copy.192
  225.9 2.9 copy.190
  228.8 8.9 %multiply_reduce_fusion.3 = (f32[1024]{0:T(1024)S(1)}, f32[1024]{0:T(1024)S(1)}, f32[1024]{0:T(1024)S(1)}, f32[1024]{0:T(1024)S(1)}, bf16[512,1024]{1,0:T(8,128)(2,1)}) fusion(f32[512,1024]{1,0:T(8,128)} %copy.192, f32[515,1024]{1,0:T(8,128)} %maximum_convert_fusion, f32[3,1024]{1,0:T(4,128)S(1)} %get-tuple-element.188, f32[1024]{0:T(1024)S(1)} %bitcast.227, ...), kind=kLoop, calls=%fused_computation.62 | loop fusion | flops 9957376 | bytes 11579392 | tf_op jit(solution)/shard_map/reduce_sum | solution.py:88
  237.7 2.9 multiply_reduce_fusion.11
  240.6 2.9 multiply_reduce_fusion.7
  243.7 59.3 %all-reduce = (f32[3,4,1024]{2,1,0:T(4,128)}, f32[1024]{0:T(1024)}) all-reduce(f32[3,4,1024]{2,1,0:T(4,128)S(1)} %pad_maximum_fusion.4, f32[1024]{0:T(1024)S(1)} %get-tuple-element.165), channel_id=1, replica_groups=mesh['ctx'=16,'head'=2] {'ctx'}, use_global_device_ids=true, to_apply=%region_21.22 | all-reduce | flops 13312 | bytes 106496 | tf_op jit(solution)/shard_map/psum | solution.py:228
  (117 shorter events, 9.8 us)
Async XLA Ops:
  7.2 9.3 %copy-start.21 = (bf16[512,1024]{1,0:T(8,128)(2,1)S(1)}, bf16[512,1024]{1,0:T(8,128)(2,1)}, u32[]{:S(2)}) copy-start(bf16[512,1024]{1,0:T(8,128)(2,1)} %param.11) | copy-start | bytes 3145732
  7.2 97.9 %all-gather.7.cloned.1.call-start = ((), (), s32[]{:S(2)}) async-start(), calls=%async_computation | async-start | bytes 8912896 | tf_op jit(solution)/shard_map/all_gather | solution.py:146
  8.8 7.1 %collective-permute-start = (bf16[3,3,1024]{2,1,0:T(4,128)(2,1)S(1)}, bf16[3,3,1024]{2,1,0:T(4,128)(2,1)S(1)}, u32[]{:S(2)}, u32[]{:S(2)}) collective-permute-start(bf16[3,3,1024]{2,1,0:T(4,128)(2,1)S(1)} %pad_maximum_fusion.5), channel_id=1, source_target_pairs={{0,2},{2,4},{4,6},{6,8},{8,10},{10,12},{12,14},{14,16},{16,18},{18... | collective-permute-start | bytes 55304 | tf_op jit(solution)/shard_map/ppermute | solution.py:18
  13.6 2.1 copy-start.24
  15.7 2.5 copy-start.22
  15.8 10.3 %copy-start.28 = (f32[8]{0:T(128)}, f32[8]{0:T(128)S(1)}, u32[]{:S(2)}) copy-start(f32[8]{0:T(128)S(1)} %exponential_multiply_fusion) | copy-start | bytes 100
  21.2 4.9 %copy-start.18 = (bf16[512,8,128]{0,2,1:T(8,128)(2,1)S(1)}, bf16[512,8,128]{0,2,1:T(8,128)(2,1)}, u32[]{:S(2)}) copy-start(bf16[512,8,128]{0,2,1:T(8,128)(2,1)} %copy.163) | copy-start | bytes 3145732
  26.1 136.6 %copy-start.8 = (bf16[64,8,8,128]{3,2,1,0:T(8,128)(2,1)}, bf16[64,8,8,128]{3,2,1,0:T(8,128)(2,1)S(1)}, u32[]{:S(2)}) copy-start(bf16[64,8,8,128]{3,2,1,0:T(8,128)(2,1)S(1)} %fusion.49) | copy-start | bytes 3145732
  27.4 165.6 %all-gather.9.cloned.1.call-start = ((), (), s32[]{:S(2)}) async-start(), calls=%async_computation.1 | async-start | bytes 4456448 | tf_op jit(solution)/shard_map/all_gather | solution.py:26
  55.2 1.3 copy-start
  60.7 1.2 copy-start.9
  60.7 1.3 copy-start.23
  60.8 1.3 copy-start.26
  61.7 3.2 %copy-start.20 = (bf16[64,8,8,128]{3,2,1,0:T(8,128)(2,1)}, bf16[64,8,8,128]{3,2,1,0:T(8,128)(2,1)S(1)}, u32[]{:S(2)}) copy-start(bf16[64,8,8,128]{3,2,1,0:T(8,128)(2,1)S(1)} %fusion.78) | copy-start | bytes 3145732
  65.0 2.0 copy-start.2
  105.1 12.5 %copy-start.10 = (bf16[512,1024]{0,1:T(8,128)(2,1)S(1)}, bf16[512,1024]{0,1:T(8,128)(2,1)}, u32[]{:S(2)}) copy-start(bf16[512,1024]{0,1:T(8,128)(2,1)} %copy.213) | copy-start | bytes 3145732
  105.1 12.5 %copy-start.13 = (f32[8,128,512]{2,1,0:T(8,128)S(1)}, f32[8,128,512]{2,1,0:T(8,128)}, u32[]{:S(2)}) copy-start(f32[8,128,512]{2,1,0:T(8,128)} %fusion.42) | copy-start | bytes 6291460
  117.6 1.9 copy-start.16
  124.7 2.9 copy-start.25
  139.0 2.3 copy-start.29
  139.0 23.6 %copy-start.27 = (f32[8,512]{1,0:T(8,128)S(1)}, f32[8,512]{1,0:T(8,128)}, u32[]{:S(2)}) copy-start(f32[8,512]{1,0:T(8,128)} %bitcast_add_fusion) | copy-start | bytes 49156
  162.7 4.1 %copy-start.19 = (bf16[512,8,128]{0,2,1:T(8,128)(2,1)S(1)}, bf16[512,8,128]{0,2,1:T(8,128)(2,1)}, u32[]{:S(2)}) copy-start(bf16[512,8,128]{0,2,1:T(8,128)(2,1)} %copy.163) | copy-start | bytes 3145732
  166.7 2.3 copy-start.3
  166.7 2.3 copy-start.12
  166.7 2.5 copy-start.17
  169.7 1.3 copy-start.5
  173.1 4.4 %copy-start.4 = (bf16[8,512,512]{2,1,0:T(8,128)(2,1)S(1)}, bf16[8,512,512]{2,1,0:T(8,128)(2,1)}, u32[]{:S(2)}) copy-start(bf16[8,512,512]{2,1,0:T(8,128)(2,1)} %copy-done.3) | copy-start | bytes 12582916
  173.1 4.4 %copy-start.11 = (bf16[512,1024]{0,1:T(8,128)(2,1)S(1)}, bf16[512,1024]{0,1:T(8,128)(2,1)}, u32[]{:S(2)}) copy-start(bf16[512,1024]{0,1:T(8,128)(2,1)} %copy.213) | copy-start | bytes 3145732
  212.9 1.3 copy-start.6
  216.8 1.3 copy-start.7
  218.4 10.3 %collective-permute-start.1 = (f32[3,3,1024]{2,1,0:T(4,128)S(1)}, f32[3,3,1024]{2,1,0:T(4,128)S(1)}, u32[]{:S(2)}, u32[]{:S(2)}) collective-permute-start(f32[3,3,1024]{2,1,0:T(4,128)S(1)} %pad_maximum_fusion.3), channel_id=1, source_target_pairs={{2,0},{4,2},{6,4},{8,6},{10,8},{12,10},{14,12},{16,14},{18,16},{20... | collective-permute-start | bytes 110600 | tf_op jit(solution)/shard_map/ppermute | solution.py:18
  228.8 8.9 %copy-start.1 = (f32[515,1024]{1,0:T(8,128)S(1)}, f32[515,1024]{1,0:T(8,128)}, u32[]{:S(2)}) copy-start(f32[515,1024]{1,0:T(8,128)} %copy-done) | copy-start | bytes 6328324
  228.8 8.9 %copy-start.15 = (f32[512,1024]{1,0:T(8,128)S(1)}, f32[512,1024]{1,0:T(8,128)}, u32[]{:S(2)}) copy-start(f32[512,1024]{1,0:T(8,128)} %copy.176) | copy-start | bytes 6291460
  237.7 3.0 copy-start.14
Sparse Core Ops, SparseCore 0:
  27.6 77.4 all-gather.6
  144.1 48.9 all-gather.8
where the time goes:
time: 311 us; the launch traced here: 310 us
  blocking collectives  111 us (36%)
  other arithmetic  55.7 us (18%)
  waiting for transfers between devices  48.9 us (16%)
  matrix products  41.3 us (13%)
  local copies, waits for them, and re-layouts  34.1 us (11%)
  between operations  14.5 us (5%)
  starting transfers between devices  3.99 us (1%)
    psum x1, blocking collectives, body(): conv_grad, gain_grad = lax.psum((conv_part, gain_part), 'ctx')  59.3 us
    all_gather x1, waiting for transfers between devices, body(): lax.all_gather(device_sum[1][None], 'ctx', axis=0, tiled=True)  35.3 us
    all_gather x1, blocking collectives, body(): all_totals = lax.all_gather(device_sum[0][None], 'ctx', axis=0, tiled=True)  22.8 us
    all_gather x1, blocking collectives, prefix(): lax.all_gather(a.astype(kind), axis)  18.6 us
    add x15, other arithmetic, chain_step(): jnp.exp(later_part[0])[..., None, None] * earlier[1] + later_part[1]  16.6 us
    reduce_sum x3, other arithmetic, conv_backward(): jnp.sum(grad_rows * extended[TAPS - 1:TAPS - 1 + tok_here], axis=0)  14.7 us
    all_gather x1, waiting for transfers between devices, prefix(): lax.all_gather(a.astype(kind), axis)  13.5 us
    dot_general x1, matrix products, body(): jnp.einsum('nh,nhde->hde', factor_table, lax.all_gather(device_sum[1][Non...  12.5 us
  transfers between devices with their start and end apart: 4, of which 2 were waited for; matrix products, arithmetic and copies ran while one was open for 14% of the time, Pallas kernels for 0%

commit v1 on v0

v1 whole, which is shorter than its diff:
```python
import functools

import jax
import jax.numpy as jnp
from jax import lax
from jax.experimental import pallas as pl
from jax.experimental.pallas import tpu as pltpu
from jax.sharding import PartitionSpec as P

HD = 128
TAPS = 4
GROUP = 512
HALF = GROUP // 2
PAD = 16
EPS = 1e-05
MESH = pl.DeviceIdType.MESH
F32 = jnp.float32
BF16 = jnp.bfloat16


def dot_nn(a, b):
    return lax.dot_general(a, b, (((1,), (0,)), ((), ())), preferred_element_type=F32)


def dot_nt(a, b):
    return lax.dot_general(a, b, (((1,), (1,)), ((), ())), preferred_element_type=F32)


def dot_tn(a, b):
    return lax.dot_general(a, b, (((0,), (0,)), ((), ())), preferred_element_type=F32)


def kernel(
    n, m, heads, owners,
    q_hbm, k_hbm, v_hbm, g_hbm, lg_ref, w_ref, gain_ref,
    mix_hbm, qg_hbm, kg_hbm, vg_hbm, cgrad_ref, ggrad_ref,
    ext, xf, qc, kc, vc, gb, att, og, mixb, outb, cg,
    w0, w1, p0, p1, colb, rowb, closb, closr,
    fs, fr, fo, fi, bs, br, bo, bi,
    accs, acci, invb, coefb, hs_tx, hs_rx,
    tap, tapr, tsum, tapo,
    loc, ha_s, ha_r, cl_s, cl_r,
    f1_s, f1_r, f2_s, f2_r, b1_s, b1_r, b2_s, b2_r,
    hs_s, hs_r, eh_s, eh_r, t1_s, t1_r, t2_s, t2_r,
):
    me = lax.axis_index("ctx")
    hme = lax.axis_index("head")
    per = owners // heads
    R = HD // per
    tiles = 2 * heads
    width = heads * HD
    total = width * m
    convs = (qc, kc, vc)

    def ctx_copy(src, dst, ss, rs, p):
        return pltpu.make_async_remote_copy(
            src_ref=src, dst_ref=dst, send_sem=ss, recv_sem=rs,
            device_id={"ctx": p}, device_id_type=MESH,
        )

    def head_copy(src, dst, ss, rs, p):
        return pltpu.make_async_remote_copy(
            src_ref=src, dst_ref=dst, send_sem=ss, recv_sem=rs,
            device_id={"head": p}, device_id_type=MESH,
        )

    def peers(count, fn):
        def one(d, c):
            p = lax.rem(me + d, n)
            if count == n:
                fn(p)
            else:
                pl.when(p < count)(lambda: fn(p))
            return c

        lax.fori_loop(1, n, one, 0)

    def owning(count, fn):
        if count == n:
            fn()
        else:
            pl.when(me < count)(fn)

    def cols_of(h):
        return pl.ds(pl.multiple_of(h * HD, HD), HD)

    ins = [
        pltpu.make_async_copy(src, ext.at[c, pl.ds(PAD, GROUP), :], loc.at[c])
        for c, src in enumerate((q_hbm, k_hbm, v_hbm))
    ]
    ins.append(pltpu.make_async_copy(g_hbm, gb, loc.at[3]))
    for cp in ins:
        cp.start()

    barrier = pltpu.get_barrier_semaphore()

    def greet(p):
        pl.semaphore_signal(barrier, inc=1, device_id={"ctx": p}, device_id_type=MESH)

    peers(n, greet)
    for d in range(1, m):
        pl.semaphore_signal(
            barrier, inc=1, device_id={"head": lax.rem(hme + d, m)}, device_id_type=MESH
        )

    run = lg_ref[...]
    lane = lax.broadcasted_iota(jnp.int32, run.shape, 1)
    d = 1
    while d < GROUP:
        run = run + jnp.where(lane >= d, pltpu.roll(run, d, 1), 0.0)
        d *= 2
    run_t = run.T
    for h in range(heads):
        colb[h] = jnp.broadcast_to(run_t[:, h : h + 1], (GROUP, HD))
        rowb[h] = jnp.broadcast_to(run[h : h + 1, :], (8, GROUP))
        closb[h] = jnp.broadcast_to(run[h : h + 1, GROUP - 1 : GROUP], (8, HD))

    tap[...] = jnp.zeros_like(tap)
    hs_tx[...] = jnp.zeros_like(hs_tx)

    pl.semaphore_wait(barrier, n - 1 + m - 1)

    rows_in = (q_hbm, k_hbm, v_hbm)

    def halo(c):
        return ctx_copy(
            rows_in[c].at[pl.ds(GROUP - PAD, PAD), :], ext.at[c, pl.ds(0, PAD), :],
            ha_s.at[c], ha_r.at[c], lax.rem(me + 1, n),
        )

    @pl.when(me < n - 1)
    def _():
        for c in (1, 2, 0):
            halo(c).start()

    @pl.when(me == 0)
    def _():
        ext[:, pl.ds(0, PAD), :] = jnp.zeros((3, PAD, width), BF16)

    def clos_copy(p, source):
        return ctx_copy(closb.at[p // per], closr.at[source], cl_s.at[p], cl_r.at[source], p)

    peers(owners, lambda p: clos_copy(p, me).start())

    def own_clos():
        closr[me] = closb[me // per]

    owning(owners, own_clos)

    def decay(h, c):
        col = colb[h]
        row = rowb[h][0:1, :]
        top = jnp.concatenate([col[:HALF]] * 2, axis=1)
        low = jnp.concatenate([col[HALF:]] * 2, axis=1)
        keep = lax.broadcasted_iota(jnp.int32, (HALF, HALF), 0) >= lax.broadcasted_iota(
            jnp.int32, (HALF, HALF), 1
        )
        w0[h] = jnp.where(keep, jnp.exp(jnp.minimum(top - row[:, :HALF], 0.0)), 0.0)
        w1[h, :, :HALF] = jnp.exp(jnp.minimum(low - row[:, :HALF], 0.0))
        w1[h, :, HALF:] = jnp.where(keep, jnp.exp(jnp.minimum(low - row[:, HALF:], 0.0)), 0.0)
        return c

    lax.fori_loop(0, heads, decay, 0)

    for cp in ins:
        cp.wait()

    @pl.when(me > 0)
    def _():
        for c in range(3):
            halo(c).wait_recv()

    def conv(c, h):
        cols = cols_of(h)
        xf[c, :, cols] = ext[c, :, cols].astype(F32)
        y = w_ref[c, 0:1, cols] * xf[c, pl.ds(PAD, GROUP), cols]
        for j in range(1, TAPS):
            y = y + w_ref[c, j : j + 1, cols] * xf[c, pl.ds(PAD - j, GROUP), cols]
        convs[c][:, cols] = y.astype(BF16)

    def shrink_of(h):
        return jnp.exp(closb[h][0:1, :] - colb[h])

    def slice_copy(src, dst, ss, rs, o, source):
        return ctx_copy(src.at[o], dst.at[source], ss.at[o], rs.at[source], o)

    def hand_out(state, h, src, dst, ss, rs):
        state = state.astype(BF16)
        for i in range(per):
            o = h * per + i
            src[o] = state[i * R : (i + 1) * R]

            @pl.when(o != me)
            def _():
                slice_copy(src, dst, ss, rs, o, me).start()

            @pl.when(o == me)
            def _():
                dst[me] = state[i * R : (i + 1) * R]

    def scan_slices(backwards, src, ss, got, rs, out, res, ss2, rs2):
        def take():
            peers(n, lambda s: slice_copy(src, got, ss, rs, 0, s).wait_recv())

            def step(i, state):
                b = n - 1 - i if backwards else i
                out[b] = state.astype(BF16)
                return jnp.exp(closr[b][0:1, :]) * state + got[b].astype(F32)

            lax.fori_loop(0, n, step, jnp.zeros((R, HD), F32))
            peers(n, lambda p: ctx_copy(out.at[p], res.at[me], ss2.at[p], rs2.at[me], p).start())
            res[me] = out[me]

        owning(owners, take)

    def await_states(out, res, ss2, rs2):
        peers(owners, lambda o: ctx_copy(out.at[0], res.at[o], ss2.at[0], rs2.at[o], o).wait_recv())

    def state_of(res, h):
        return res[pl.ds(h * per, per)].reshape(HD, HD)

    def local_state(i, c):
        h = lax.rem(i + me, heads)
        cols = cols_of(h)
        conv(1, h)
        conv(2, h)
        ks = (kc[:, cols].astype(F32) * shrink_of(h)).astype(BF16)
        hand_out(dot_tn(ks, vc[:, cols]), h, fs, fr, f1_s, f1_r)
        return c

    lax.fori_loop(0, heads, local_state, 0)

    def inner(h, c):
        cols = cols_of(h)
        conv(0, h)
        q0, q1 = qc[:HALF, cols], qc[HALF:, cols]
        a0 = (dot_nt(q0, kc[:HALF, cols]) * w0[h]).astype(BF16)
        a1 = (dot_nt(q1, kc[:, cols]) * w1[h]).astype(BF16)
        p0[h] = a0
        p1[h] = a1
        att[:HALF, cols] = dot_nn(a0, vc[:HALF, cols])
        att[HALF:, cols] = dot_nn(a1, vc[:, cols])
        return c

    lax.fori_loop(0, heads // 2, inner, 0)

    def clos_in():
        peers(n, lambda s: clos_copy(me, s).wait_recv())

    owning(owners, clos_in)
    scan_slices(False, fs, f1_s, fr, f1_r, fo, fi, f2_s, f2_r)
    lax.fori_loop(heads // 2, heads, inner, 0)
    await_states(fo, fi, f2_s, f2_r)

    accs[...] = jnp.zeros_like(accs)
    acci[...] = jnp.zeros_like(acci)

    def outer(h, c):
        cols = cols_of(h)
        a = att[:, cols] + dot_nn(qc[:, cols], state_of(fi, h)) * jnp.exp(colb[h])
        att[:, cols] = a
        accs[...] += a * a
        acci[...] += gb[:, cols].astype(F32) * gain_ref[0:1, cols] * a
        return c

    lax.fori_loop(0, heads, outer, 0)
    hs_tx[0:1, :] = jnp.sum(accs[...].T, axis=0, keepdims=True)
    hs_tx[1:2, :] = jnp.sum(acci[...].T, axis=0, keepdims=True)

    def sums_copy(p, source):
        return head_copy(hs_tx, hs_rx.at[source], hs_s.at[p], hs_r.at[source], p)

    for d in range(1, m):
        sums_copy(lax.rem(hme + d, m), hme).start()
    hs_rx[hme] = hs_tx[...]
    for d in range(1, m):
        sums_copy(hme, lax.rem(hme + d, m)).wait_recv()
    sums = hs_rx[0]
    for d in range(1, m):
        sums = sums + hs_rx[d]
    inverse = lax.rsqrt(sums[0:1, :] / total + EPS)
    coef = inverse * inverse * (sums[1:2, :] / total)
    both = jnp.concatenate([inverse, coef, jnp.zeros((6, GROUP), F32)], axis=0).T
    invb[...] = jnp.broadcast_to(both[:, 0:1], (GROUP, HD))
    coefb[...] = jnp.broadcast_to(both[:, 1:2], (GROUP, HD))

    def norm(i, c):
        h = lax.rem(i + me, heads)
        cols = cols_of(h)
        a = att[:, cols]
        inv = invb[...]
        normed = a * inv
        gain = gain_ref[0:1, cols]
        gw = gb[:, cols].astype(F32)
        mixb[:, cols] = (normed * gain).astype(BF16)
        tap[heads + h, 4:5, :] = jnp.sum(gw * normed, axis=0, keepdims=True)
        o = (inv * (gw * gain - a * coefb[...])).astype(BF16)
        og[:, cols] = o
        qs = (qc[:, cols].astype(F32) * jnp.exp(colb[h])).astype(BF16)
        hand_out(dot_tn(qs, o), h, bs, br, b1_s, b1_r)
        return c

    lax.fori_loop(0, heads, norm, 0)
    mix_out = pltpu.make_async_copy(mixb, mix_hbm, loc.at[4])
    mix_out.start()

    def back(h, c):
        cols = cols_of(h)
        o0, o1 = og[:HALF, cols], og[HALF:, cols]
        s0 = (dot_nt(o0, vc[:HALF, cols]) * w0[h]).astype(BF16)
        s1 = (dot_nt(o1, vc[:, cols]) * w1[h]).astype(BF16)
        through = dot_nt(og[:, cols], state_of(fi, h)) * jnp.exp(colb[h])
        cg[0, :HALF, cols] = dot_nn(s0, kc[:HALF, cols]) + through[:HALF]
        cg[0, HALF:GROUP, cols] = dot_nn(s1, kc[:, cols]) + through[HALF:]
        kk = dot_tn(s1, qc[HALF:, cols])
        cg[1, :HALF, cols] = kk[:HALF] + dot_tn(s0, qc[:HALF, cols])
        cg[1, HALF:GROUP, cols] = kk[HALF:]
        vv = dot_tn(p1[h], o1)
        cg[2, :HALF, cols] = vv[:HALF] + dot_tn(p0[h], o0)
        cg[2, HALF:GROUP, cols] = vv[HALF:]
        return c

    lax.fori_loop(0, heads // 2, back, 0)
    scan_slices(True, bs, b1_s, br, b1_r, bo, bi, b2_s, b2_r)
    lax.fori_loop(heads // 2, heads, back, 0)

    def edge(c):
        return ctx_copy(
            cg.at[c, pl.ds(0, 8), :], cg.at[c, pl.ds(GROUP, 8), :],
            eh_s.at[c], eh_r.at[c], lax.rem(me + n - 1, n),
        )

    @pl.when(me == n - 1)
    def _():
        cg[:, pl.ds(GROUP, 8), :] = jnp.zeros((3, 8, width), F32)

    @pl.when(me > 0)
    def _():
        edge(0).start()

    def taps(c, h):
        cols = cols_of(h)
        part = cg[c, :GROUP, cols]
        for j in range(TAPS):
            r = c * TAPS + j
            tap[(r // 8) * heads + h, r % 8 : r % 8 + 1, :] = jnp.sum(
                part * xf[c, pl.ds(PAD - j, GROUP), cols], axis=0, keepdims=True
            )

    def q_taps(h, c):
        taps(0, h)
        return c

    lax.fori_loop(0, heads, q_taps, 0)
    await_states(bo, bi, b2_s, b2_r)

    def late(h, c):
        cols = cols_of(h)
        state = state_of(bi, h)
        sh = shrink_of(h)
        cg[1, :GROUP, cols] += dot_nt(vc[:, cols], state) * sh
        cg[2, :GROUP, cols] += dot_nn(kc[:, cols], state) * sh
        return c

    lax.fori_loop(0, heads, late, 0)

    @pl.when(me > 0)
    def _():
        edge(1).start()
        edge(2).start()

    def kv_taps(h, c):
        taps(1, h)
        taps(2, h)
        return c

    lax.fori_loop(0, heads, kv_taps, 0)

    def tap_copy(o, source):
        return ctx_copy(tap.at[o], tapr.at[source], t1_s.at[o], t1_r.at[source], o)

    peers(tiles, lambda o: tap_copy(o, me).start())

    @pl.when(me < n - 1)
    def _():
        for c in range(3):
            edge(c).wait_recv()

    def unconv(c):
        def one(h, carry):
            cols = cols_of(h)
            y = w_ref[c, 0:1, cols] * cg[c, pl.ds(0, GROUP), cols]
            for j in range(1, TAPS):
                y = y + w_ref[c, j : j + 1, cols] * cg[c, pl.ds(j, GROUP), cols]
            outb[c, :, cols] = y.astype(BF16)
            return carry

        lax.fori_loop(0, heads, one, 0)

    outs = [
        pltpu.make_async_copy(outb.at[c], dst, loc.at[5 + c])
        for c, dst in enumerate((qg_hbm, kg_hbm, vg_hbm))
    ]
    unconv(0)
    outs[0].start()

    def sum_copy(p, source):
        return ctx_copy(tsum, tapo.at[source], t2_s.at[p], t2_r.at[source], p)

    def own_sum():
        tapr[me] = tap[me]
        peers(n, lambda s: tap_copy(0, s).wait_recv())
        tsum[...] = lax.fori_loop(0, n, lambda s, a: a + tapr[s], jnp.zeros((8, HD), F32))
        tapo[me] = tsum[...]
        peers(n, lambda p: sum_copy(p, me).start())

    owning(tiles, own_sum)
    unconv(1)
    outs[1].start()
    unconv(2)
    outs[2].start()
    peers(tiles, lambda o: sum_copy(0, o).wait_recv())
    for h in range(heads):
        cols = slice(h * HD, (h + 1) * HD)
        low, high = tapo[h], tapo[heads + h]
        cgrad_ref[0, :, cols] = low[0:4]
        cgrad_ref[1, :, cols] = low[4:8]
        cgrad_ref[2, :, cols] = high[0:4]
        ggrad_ref[0:1, cols] = high[4:5]

    @pl.when(me < n - 1)
    def _():
        for c in range(3):
            halo(c).wait_send()

    @pl.when(me > 0)
    def _():
        for c in range(3):
            edge(c).wait_send()

    def sent_to_owner(o):
        clos_copy(o, me).wait_send()
        slice_copy(fs, fr, f1_s, f1_r, o, me).wait_send()
        slice_copy(bs, br, b1_s, b1_r, o, me).wait_send()

    peers(owners, sent_to_owner)

    def sent_states():
        def one(p):
            ctx_copy(fo.at[p], fi.at[me], f2_s.at[p], f2_r.at[me], p).wait_send()
            ctx_copy(bo.at[p], bi.at[me], b2_s.at[p], b2_r.at[me], p).wait_send()

        peers(n, one)

    owning(owners, sent_states)
    for d in range(1, m):
        sums_copy(lax.rem(hme + d, m), hme).wait_send()
    peers(tiles, lambda o: tap_copy(o, me).wait_send())
    owning(tiles, lambda: peers(n, lambda p: sum_copy(p, me).wait_send()))
    mix_out.wait()
    for cp in outs:
        cp.wait()


def body(n, m, query_rows, key_rows, value_rows, log_gate, conv_weight, norm_gain, mixed_grad):
    tok_here, width = query_rows.shape
    assert tok_here == GROUP
    heads = width // HD
    owners = min(n, width // 16)
    per = owners // heads
    R = HD // per
    tiles = 2 * heads
    assert tiles <= n
    if heads < 8:
        log_gate = jnp.pad(log_gate, ((0, 8 - heads), (0, 0)))
    any_ = pl.BlockSpec(memory_space=pl.ANY)
    vm = pl.BlockSpec(memory_space=pltpu.VMEM)
    V = pltpu.VMEM
    S = pltpu.SemaphoreType.DMA
    rows = jax.ShapeDtypeStruct((GROUP, width), BF16)
    result = pl.pallas_call(
        functools.partial(kernel, n, m, heads, owners),
        out_shape=(
            rows, rows, rows, rows,
            jax.ShapeDtypeStruct((3, TAPS, width), F32),
            jax.ShapeDtypeStruct((1, width), F32),
        ),
        in_specs=[any_] * 4 + [vm] * 3,
        out_specs=(any_, any_, any_, any_, vm, vm),
        scratch_shapes=[
            V((3, PAD + GROUP, width), BF16),
            V((3, PAD + GROUP, width), F32),
            V((GROUP, width), BF16),
            V((GROUP, width), BF16),
            V((GROUP, width), BF16),
            V((GROUP, width), BF16),
            V((GROUP, width), F32),
            V((GROUP, width), BF16),
            V((GROUP, width), BF16),
            V((3, GROUP, width), BF16),
            V((3, GROUP + 8, width), F32),
            V((heads, HALF, HALF), F32),
            V((heads, HALF, GROUP), F32),
            V((heads, HALF, HALF), BF16),
            V((heads, HALF, GROUP), BF16),
            V((heads, GROUP, HD), F32),
            V((heads, 8, GROUP), F32),
            V((heads, 8, HD), F32),
            V((n, 8, HD), F32),
            V((owners, R, HD), BF16),
            V((n, R, HD), BF16),
            V((n, R, HD), BF16),
            V((owners, R, HD), BF16),
            V((owners, R, HD), BF16),
            V((n, R, HD), BF16),
            V((n, R, HD), BF16),
            V((owners, R, HD), BF16),
            V((GROUP, HD), F32),
            V((GROUP, HD), F32),
            V((GROUP, HD), F32),
            V((GROUP, HD), F32),
            V((8, GROUP), F32),
            V((m, 8, GROUP), F32),
            V((tiles, 8, HD), F32),
            V((n, 8, HD), F32),
            V((8, HD), F32),
            V((tiles, 8, HD), F32),
            S((8,)), S((3,)), S((3,)), S((n,)), S((n,)),
            S((n,)), S((n,)), S((n,)), S((n,)),
            S((n,)), S((n,)), S((n,)), S((n,)),
            S((m,)), S((m,)), S((3,)), S((3,)),
            S((n,)), S((n,)), S((n,)), S((n,)),
        ],
        compiler_params=pltpu.CompilerParams(
            collective_id=0, has_side_effects=True, vmem_limit_bytes=60 * 1024 * 1024
        ),
    )(
        query_rows, key_rows, value_rows, mixed_grad,
        log_gate, conv_weight, norm_gain.reshape(1, width),
    )
    return (*result[:5], result[5].reshape(width))


def solution(mesh):
    n, m = mesh.shape["ctx"], mesh.shape["head"]
    rows = P("ctx", "head")
    return jax.shard_map(
        functools.partial(body, n, m),
        mesh=mesh,
        in_specs=(rows, rows, rows, P("head", "ctx"), P(None, None, "head"), P("head"), rows),
        out_specs=(rows, rows, rows, rows, P(None, None, "head"), P("head")),
        check_vma=False,
    )
```

time: 311 us -> 73.4 us (0.24)
  blocking collectives: 111 us -> 0 us
  Pallas kernels: 0 us -> 64.6 us
  other arithmetic: 55.7 us -> 0 us
  waiting for transfers between devices: 48.9 us -> 0 us
  matrix products: 41.3 us -> 0 us
  local copies, waits for them, and re-layouts: 34.1 us -> 7.8 us
  between operations: 14.5 us -> 0.66 us
  starting transfers between devices: 3.99 us -> 0 us
    psum x3 -> x0, blocking collectives: 69.4 us -> none  [the longest x1 59.3 us: body(): conv_grad, gain_grad = lax.psum((conv_part, gain_part), 'ctx')]
    pallas_call x0 -> x1, Pallas kernels: none -> 64.6 us  [body(): pl.pallas_call(functools.partial(kernel, n, m, heads, owners), out_shape=...]
    all_gather x2 -> x0, waiting for transfers between devices: 48.9 us -> none  [the longest x1 35.3 us: body(): lax.all_gather(device_sum[1][None], 'ctx', axis=0, tiled=True)]
    all_gather x2 -> x0, blocking collectives: 41.4 us -> none  [the longest x1 22.8 us: body(): all_totals = lax.all_gather(device_sum[0][None], 'ctx', axis=0, tiled=True)]
    dot_general x13 -> x0, matrix products: 41.3 us -> none  [the longest x1 12.5 us: body(): jnp.einsum('nh,nhde->hde', factor_table, lax.all_gather(device_sum[1][Non...]
    reduce_sum x4 -> x0, other arithmetic: 17.4 us -> none  [the longest x3 14.7 us: conv_backward(): jnp.sum(grad_rows * extended[TAPS - 1:TAPS - 1 + tok_here], axis=0)]
    add x15 -> x0, other arithmetic: 16.6 us -> none  [chain_step(): jnp.exp(later_part[0])[..., None, None] * earlier[1] + later_part[1]]
    reshape x4 -> x0, local copies, waits for them, and re-layouts: 11.7 us -> none  [the longest x1 2.95 us: body(): query_cg = query_cg.reshape(tok_here, width_here)]
  transfers between devices with their start and end apart: 4 -> 0, of which waited for: 2 -> 0; matrix products, arithmetic and copies ran while one was open for 14% -> 0% of each run, Pallas kernels for 0% -> 0%
where the time goes in v1:
time: 73.4 us; the launch traced here: 73 us
  Pallas kernels  64.6 us (88%)
  local copies, waits for them, and re-layouts  7.8 us (11%)
    pallas_call x1, Pallas kernels, body(): pl.pallas_call(functools.partial(kernel, n, m, heads, owners), out_shape=...  64.6 us
    unnamed x16, local copies, waits for them, and re-layouts  7.8 us

profile of v1, /device:TPU:0, one launch (start us, length us, event | category | flops | bytes accessed | tf_op | source)
XLA Modules:
  0.0 73.0 jit_solution(11441482556245698081)
XLA Ops:
  0.6 64.6 %shard_map.118 = (bf16[512,1024]{1,0:T(8,128)(2,1)}, bf16[512,1024]{1,0:T(8,128)(2,1)}, bf16[512,1024]{1,0:T(8,128)(2,1)}, bf16[512,1024]{1,0:T(8,128)(2,1)}, f32[3,4,1024]{2,1,0:T(4,128)}, /*index=5*/f32[1,1024]{1,0:T(1,128)}) custom-call(bf16[512,1024]{1,0:T(8,128)(2,1)} %q_hbm.1, bf16[512,1024]{1,0:T(8,128)(2,1)} %k_hbm.1, bf16[512,1024]{1,0:T(8,128)(2,1)} %v_hbm.1, ...), custom_call_target="tpu_custom_call" | custom-call | tf_op jit(solution)/shard_map/pallas_call | solution.py:481
  65.2 0.0 copy-start.2
  65.2 2.4 %copy.19 = bf16[512,1024]{1,0:T(8,128)(2,1)} copy(bf16[512,1024]{1,0:T(8,128)(2,1)} %get-tuple-element.24) | data formatting | bytes 2097152
  67.6 0.0 copy-done.2
  67.6 0.0 copy-start.1
  67.6 1.0 %copy.20 = bf16[512,1024]{1,0:T(8,128)(2,1)} copy(bf16[512,1024]{1,0:T(8,128)(2,1)S(1)} %copy-done.2) | data formatting | bytes 2097152
  68.6 0.6 copy-done.1
  69.2 0.0 copy-start
  69.2 1.0 %copy.21 = bf16[512,1024]{1,0:T(8,128)(2,1)} copy(bf16[512,1024]{1,0:T(8,128)(2,1)S(1)} %copy-done.1) | data formatting | bytes 2097152
  70.2 0.6 copy-done
  70.8 0.0 copy-start.3
  70.8 1.0 %copy.22 = bf16[512,1024]{1,0:T(8,128)(2,1)} copy(bf16[512,1024]{1,0:T(8,128)(2,1)S(1)} %copy-done) | data formatting | bytes 2097152
  71.8 0.0 copy-done.3
  71.8 0.0 copy-start.4
  71.8 0.6 copy.23
  72.4 0.1 copy-done.4
  72.5 0.6 copy.24
Async XLA Ops:
  65.2 2.4 %copy-start.2 = (bf16[512,1024]{1,0:T(8,128)(2,1)S(1)}, bf16[512,1024]{1,0:T(8,128)(2,1)}, u32[]{:S(2)}) copy-start(bf16[512,1024]{1,0:T(8,128)(2,1)} %get-tuple-element.25) | copy-start | bytes 3145732
  67.6 1.6 %copy-start.1 = (bf16[512,1024]{1,0:T(8,128)(2,1)S(1)}, bf16[512,1024]{1,0:T(8,128)(2,1)}, u32[]{:S(2)}) copy-start(bf16[512,1024]{1,0:T(8,128)(2,1)} %get-tuple-element.26) | copy-start | bytes 3145732
  69.2 1.6 %copy-start = (bf16[512,1024]{1,0:T(8,128)(2,1)S(1)}, bf16[512,1024]{1,0:T(8,128)(2,1)}, u32[]{:S(2)}) copy-start(bf16[512,1024]{1,0:T(8,128)(2,1)} %get-tuple-element.27) | copy-start | bytes 3145732
  70.8 1.0 %copy-start.3 = (f32[3,4,1024]{2,1,0:T(4,128)S(1)}, f32[3,4,1024]{2,1,0:T(4,128)}, u32[]{:S(2)}) copy-start(f32[3,4,1024]{2,1,0:T(4,128)} %get-tuple-element.28) | copy-start | bytes 147460
  71.8 0.7 copy-start.4

commit v2 on v1

--- a/solution.py
+++ b/solution.py
@@ -11,6 +11,7 @@
 TAPS = 4
 GROUP = 512
 HALF = GROUP // 2
+UNROLL = 8
 PAD = 16
 EPS = 1e-05
 MESH = pl.DeviceIdType.MESH
@@ -82,7 +83,23 @@
             pl.when(me < count)(fn)
 
     def cols_of(h):
+        if isinstance(h, int):
+            return pl.ds(h * HD, HD)
         return pl.ds(pl.multiple_of(h * HD, HD), HD)
+
+    def over(lo, hi, fn):
+        k = min(UNROLL, hi - lo)
+        if k == hi - lo:
+            for h in range(lo, hi):
+                fn(h, 0)
+        else:
+
+            def some(i, c):
+                for u in range(k):
+                    fn(lo + i * k + u, 0)
+                return c
+
+            lax.fori_loop(0, (hi - lo) // k, some, 0)
 
     ins = [
         pltpu.make_async_copy(src, ext.at[c, pl.ds(PAD, GROUP), :], loc.at[c])
@@ -118,13 +135,13 @@
     tap[...] = jnp.zeros_like(tap)
     hs_tx[...] = jnp.zeros_like(hs_tx)
 
+    for cp in ins:
+        cp.wait()
     pl.semaphore_wait(barrier, n - 1 + m - 1)
-
-    rows_in = (q_hbm, k_hbm, v_hbm)
 
     def halo(c):
         return ctx_copy(
-            rows_in[c].at[pl.ds(GROUP - PAD, PAD), :], ext.at[c, pl.ds(0, PAD), :],
+            ext.at[c, pl.ds(GROUP, PAD), :], ext.at[c, pl.ds(0, PAD), :],
             ha_s.at[c], ha_r.at[c], lax.rem(me + 1, n),
         )
 
@@ -160,10 +177,7 @@
         w1[h, :, HALF:] = jnp.where(keep, jnp.exp(jnp.minimum(low - row[:, HALF:], 0.0)), 0.0)
         return c
 
-    lax.fori_loop(0, heads, decay, 0)
-
-    for cp in ins:
-        cp.wait()
+    over(0, heads, decay)
 
     @pl.when(me > 0)
     def _():
@@ -184,11 +198,16 @@
     def slice_copy(src, dst, ss, rs, o, source):
         return ctx_copy(src.at[o], dst.at[source], ss.at[o], rs.at[source], o)
 
-    def hand_out(state, h, src, dst, ss, rs):
+    def keep_slices(state, h, src):
         state = state.astype(BF16)
         for i in range(per):
-            o = h * per + i
-            src[o] = state[i * R : (i + 1) * R]
+            src[h * per + i] = state[i * R : (i + 1) * R]
+
+    def hand_out(lo, hi, src, dst, ss, rs):
+        span = (hi - lo) * per
+
+        def one(d, c):
+            o = lo * per + lax.rem(d + me, span)
 
             @pl.when(o != me)
             def _():
@@ -196,7 +215,11 @@
 
             @pl.when(o == me)
             def _():
-                dst[me] = state[i * R : (i + 1) * R]
+                dst[me] = src[me]
+
+            return c
+
+        lax.fori_loop(0, span, one, 0)
 
     def scan_slices(backwards, src, ss, got, rs, out, res, ss2, rs2):
         def take():
@@ -219,16 +242,19 @@
     def state_of(res, h):
         return res[pl.ds(h * per, per)].reshape(HD, HD)
 
-    def local_state(i, c):
-        h = lax.rem(i + me, heads)
+    def local_state(h, c):
         cols = cols_of(h)
         conv(1, h)
         conv(2, h)
         ks = (kc[:, cols].astype(F32) * shrink_of(h)).astype(BF16)
-        hand_out(dot_tn(ks, vc[:, cols]), h, fs, fr, f1_s, f1_r)
-        return c
-
-    lax.fori_loop(0, heads, local_state, 0)
+        keep_slices(dot_tn(ks, vc[:, cols]), h, fs)
+        return c
+
+    mid = heads // 2
+    over(0, mid, local_state)
+    hand_out(0, mid, fs, fr, f1_s, f1_r)
+    over(mid, heads, local_state)
+    hand_out(mid, heads, fs, fr, f1_s, f1_r)
 
     def inner(h, c):
         cols = cols_of(h)
@@ -242,14 +268,14 @@
         att[HALF:, cols] = dot_nn(a1, vc[:, cols])
         return c
 
-    lax.fori_loop(0, heads // 2, inner, 0)
+    over(0, mid, inner)
 
     def clos_in():
         peers(n, lambda s: clos_copy(me, s).wait_recv())
 
     owning(owners, clos_in)
     scan_slices(False, fs, f1_s, fr, f1_r, fo, fi, f2_s, f2_r)
-    lax.fori_loop(heads // 2, heads, inner, 0)
+    over(mid, heads, inner)
     await_states(fo, fi, f2_s, f2_r)
 
     accs[...] = jnp.zeros_like(accs)
@@ -263,7 +289,7 @@
         acci[...] += gb[:, cols].astype(F32) * gain_ref[0:1, cols] * a
         return c
 
-    lax.fori_loop(0, heads, outer, 0)
+    over(0, heads, outer)
     hs_tx[0:1, :] = jnp.sum(accs[...].T, axis=0, keepdims=True)
     hs_tx[1:2, :] = jnp.sum(acci[...].T, axis=0, keepdims=True)
 
@@ -284,8 +310,7 @@
     invb[...] = jnp.broadcast_to(both[:, 0:1], (GROUP, HD))
     coefb[...] = jnp.broadcast_to(both[:, 1:2], (GROUP, HD))
 
-    def norm(i, c):
-        h = lax.rem(i + me, heads)
+    def norm(h, c):
         cols = cols_of(h)
         a = att[:, cols]
         inv = invb[...]
@@ -297,10 +322,13 @@
         o = (inv * (gw * gain - a * coefb[...])).astype(BF16)
         og[:, cols] = o
         qs = (qc[:, cols].astype(F32) * jnp.exp(colb[h])).astype(BF16)
-        hand_out(dot_tn(qs, o), h, bs, br, b1_s, b1_r)
-        return c
-
-    lax.fori_loop(0, heads, norm, 0)
+        keep_slices(dot_tn(qs, o), h, bs)
+        return c
+
+    over(0, mid, norm)
+    hand_out(0, mid, bs, br, b1_s, b1_r)
+    over(mid, heads, norm)
+    hand_out(mid, heads, bs, br, b1_s, b1_r)
     mix_out = pltpu.make_async_copy(mixb, mix_hbm, loc.at[4])
     mix_out.start()
 
@@ -320,9 +348,9 @@
         cg[2, HALF:GROUP, cols] = vv[HALF:]
         return c
 
-    lax.fori_loop(0, heads // 2, back, 0)
+    over(0, mid, back)
     scan_slices(True, bs, b1_s, br, b1_r, bo, bi, b2_s, b2_r)
-    lax.fori_loop(heads // 2, heads, back, 0)
+    over(mid, heads, back)
 
     def edge(c):
         return ctx_copy(
@@ -351,7 +379,7 @@
         taps(0, h)
         return c
 
-    lax.fori_loop(0, heads, q_taps, 0)
+    over(0, heads, q_taps)
     await_states(bo, bi, b2_s, b2_r)
 
     def late(h, c):
@@ -362,7 +390,7 @@
         cg[2, :GROUP, cols] += dot_nn(kc[:, cols], state) * sh
         return c
 
-    lax.fori_loop(0, heads, late, 0)
+    over(0, heads, late)
 
     @pl.when(me > 0)
     def _():
@@ -374,7 +402,7 @@
         taps(2, h)
         return c
 
-    lax.fori_loop(0, heads, kv_taps, 0)
+    over(0, heads, kv_taps)
 
     def tap_copy(o, source):
         return ctx_copy(tap.at[o], tapr.at[source], t1_s.at[o], t1_r.at[source], o)
@@ -395,7 +423,7 @@
             outb[c, :, cols] = y.astype(BF16)
             return carry
 
-        lax.fori_loop(0, heads, one, 0)
+        over(0, heads, one)
 
     outs = [
         pltpu.make_async_copy(outb.at[c], dst, loc.at[5 + c])
@@ -460,6 +488,36 @@
     mix_out.wait()
     for cp in outs:
         cp.wait()
+
+
+PIECES = 4
+
+
+def hand_on(*refs):
+    count = (len(refs) - 3) // 2
+    srcs, dsts = refs[:count], refs[count : 2 * count]
+    stage, got, put = refs[-3:]
+    step = GROUP // PIECES
+    loads, stores = [], []
+    for j in range(PIECES):
+        part = pl.ds(j * step, step)
+        for i in range(4):
+            k = i * PIECES + j
+            loads.append(
+                pltpu.make_async_copy(srcs[i].at[part, :], stage.at[i, part, :], got.at[k])
+            )
+            stores.append(
+                pltpu.make_async_copy(stage.at[i, part, :], dsts[i].at[part, :], put.at[k])
+            )
+    for cp in loads:
+        cp.start()
+    for i in range(4, count):
+        dsts[i][...] = srcs[i][...]
+    for cp, out in zip(loads, stores):
+        cp.wait()
+        out.start()
+    for out in stores:
+        out.wait()
 
 
 def body(n, m, query_rows, key_rows, value_rows, log_gate, conv_weight, norm_gain, mixed_grad):
@@ -538,6 +596,14 @@
         query_rows, key_rows, value_rows, mixed_grad,
         log_gate, conv_weight, norm_gain.reshape(1, width),
     )
+    specs = [any_] * 4 + [vm] * 2
+    result = pl.pallas_call(
+        hand_on,
+        out_shape=tuple(jax.ShapeDtypeStruct(r.shape, r.dtype) for r in result),
+        in_specs=specs,
+        out_specs=tuple(specs),
+        scratch_shapes=[V((4, GROUP, width), BF16), S((4 * PIECES,)), S((4 * PIECES,))],
+    )(*result)
     return (*result[:5], result[5].reshape(width))
 
 

time: 73.4 us -> 71.1 us (0.969)
  local copies, waits for them, and re-layouts: 7.8 us -> 0 us
  Pallas kernels: 64.6 us -> 70 us
    unnamed x16 -> x0, local copies, waits for them, and re-layouts: 7.8 us -> none
    pallas_call x0 -> x1, Pallas kernels: none -> 5.27 us  [body(): pl.pallas_call(hand_on, out_shape=tuple((jax.ShapeDtypeStruct(r.shape, r....]
where the time goes in v2:
time: 71.1 us; the launch traced here: 70.8 us
  Pallas kernels  70 us (98%)
  between operations  0.8 us (1%)
    pallas_call x1, Pallas kernels, body(): pl.pallas_call(functools.partial(kernel, n, m, heads, owners), out_shape=...  64.7 us
    pallas_call x1, Pallas kernels, body(): pl.pallas_call(hand_on, out_shape=tuple((jax.ShapeDtypeStruct(r.shape, r....  5.27 us

profile of v2, /device:TPU:0, one launch (start us, length us, event | category | flops | bytes accessed | tf_op | source)
XLA Modules:
  0.0 70.8 jit_solution(9268636418653941462)
XLA Ops:
  0.6 64.7 %shard_map.118 = (bf16[512,1024]{1,0:T(8,128)(2,1)}, bf16[512,1024]{1,0:T(8,128)(2,1)}, bf16[512,1024]{1,0:T(8,128)(2,1)}, bf16[512,1024]{1,0:T(8,128)(2,1)}, f32[3,4,1024]{2,1,0:T(4,128)}, /*index=5*/f32[1,1024]{1,0:T(1,128)}) custom-call(bf16[512,1024]{1,0:T(8,128)(2,1)} %q_hbm.1, bf16[512,1024]{1,0:T(8,128)(2,1)} %k_hbm.1, bf16[512,1024]{1,0:T(8,128)(2,1)} %v_hbm.1, ...), custom_call_target="tpu_custom_call" | custom-call | tf_op jit(solution)/shard_map/pallas_call | solution.py:539
  65.4 5.3 %shard_map.119 = (bf16[512,1024]{1,0:T(8,128)(2,1)}, bf16[512,1024]{1,0:T(8,128)(2,1)}, bf16[512,1024]{1,0:T(8,128)(2,1)}, bf16[512,1024]{1,0:T(8,128)(2,1)}, f32[3,4,1024]{2,1,0:T(4,128)}, /*index=5*/f32[1,1024]{1,0:T(1,128)}) custom-call(bf16[512,1024]{1,0:T(8,128)(2,1)} %get-tuple-element.18.refs_0_, bf16[512,1024]{1,0:T(8,128)(2,1)} %get-tuple-element.19.refs_1_, ...), custom_call_target="tpu_custom_call" | custom-call | tf_op jit(solution)/shard_map/pallas_call | solution.py:600

commit v3 on v2

--- a/solution.py
+++ b/solution.py
@@ -177,7 +177,7 @@
         w1[h, :, HALF:] = jnp.where(keep, jnp.exp(jnp.minimum(low - row[:, HALF:], 0.0)), 0.0)
         return c
 
-    over(0, heads, decay)
+    over(0, heads // 2, decay)
 
     @pl.when(me > 0)
     def _():
@@ -255,6 +255,7 @@
     hand_out(0, mid, fs, fr, f1_s, f1_r)
     over(mid, heads, local_state)
     hand_out(mid, heads, fs, fr, f1_s, f1_r)
+    over(mid, heads, decay)
 
     def inner(h, c):
         cols = cols_of(h)
@@ -380,39 +381,10 @@
         return c
 
     over(0, heads, q_taps)
-    await_states(bo, bi, b2_s, b2_r)
-
-    def late(h, c):
-        cols = cols_of(h)
-        state = state_of(bi, h)
-        sh = shrink_of(h)
-        cg[1, :GROUP, cols] += dot_nt(vc[:, cols], state) * sh
-        cg[2, :GROUP, cols] += dot_nn(kc[:, cols], state) * sh
-        return c
-
-    over(0, heads, late)
-
-    @pl.when(me > 0)
-    def _():
-        edge(1).start()
-        edge(2).start()
-
-    def kv_taps(h, c):
-        taps(1, h)
-        taps(2, h)
-        return c
-
-    over(0, heads, kv_taps)
-
-    def tap_copy(o, source):
-        return ctx_copy(tap.at[o], tapr.at[source], t1_s.at[o], t1_r.at[source], o)
-
-    peers(tiles, lambda o: tap_copy(o, me).start())
 
     @pl.when(me < n - 1)
     def _():
-        for c in range(3):
-            edge(c).wait_recv()
+        edge(0).wait_recv()
 
     def unconv(c):
         def one(h, carry):
@@ -431,6 +403,42 @@
     ]
     unconv(0)
     outs[0].start()
+    await_states(bo, bi, b2_s, b2_r)
+
+    def late(h, c):
+        cols = cols_of(h)
+        state = state_of(bi, h)
+        sh = shrink_of(h)
+        cg[1, :GROUP, cols] += dot_nt(vc[:, cols], state) * sh
+        cg[2, :GROUP, cols] += dot_nn(kc[:, cols], state) * sh
+        return c
+
+    over(0, heads, late)
+
+    @pl.when(me > 0)
+    def _():
+        edge(1).start()
+        edge(2).start()
+
+    def kv_taps(h, c):
+        taps(1, h)
+        taps(2, h)
+        return c
+
+    over(0, heads, kv_taps)
+
+    def tap_copy(o, source):
+        return ctx_copy(tap.at[o], tapr.at[source], t1_s.at[o], t1_r.at[source], o)
+
+    peers(tiles, lambda o: tap_copy(o, me).start())
+
+    @pl.when(me < n - 1)
+    def _():
+        for c in (1, 2):
+            edge(c).wait_recv()
+
+    unconv(1)
+    outs[1].start()
 
     def sum_copy(p, source):
         return ctx_copy(tsum, tapo.at[source], t2_s.at[p], t2_r.at[source], p)
@@ -443,8 +451,6 @@
         peers(n, lambda p: sum_copy(p, me).start())
 
     owning(tiles, own_sum)
-    unconv(1)
-    outs[1].start()
     unconv(2)
     outs[2].start()
     peers(tiles, lambda o: sum_copy(0, o).wait_recv())

time: 71.1 us -> 71.5 us (level)
  no operation moved by 1% of the time
where the time goes in v3:
time: 71.5 us; the launch traced here: 71.3 us
  Pallas kernels  70.5 us (99%)
  between operations  0.8 us (1%)
    pallas_call x1, Pallas kernels, body(): pl.pallas_call(functools.partial(kernel, n, m, heads, owners), out_shape=...  65.2 us
    pallas_call x1, Pallas kernels, body(): pl.pallas_call(hand_on, out_shape=tuple((jax.ShapeDtypeStruct(r.shape, r....  5.27 us

profile of v3, /device:TPU:0, one launch (start us, length us, event | category | flops | bytes accessed | tf_op | source)
XLA Modules:
  0.0 71.3 jit_solution(3267107485770581935)
XLA Ops:
  0.6 65.2 %shard_map.118 = (bf16[512,1024]{1,0:T(8,128)(2,1)}, bf16[512,1024]{1,0:T(8,128)(2,1)}, bf16[512,1024]{1,0:T(8,128)(2,1)}, bf16[512,1024]{1,0:T(8,128)(2,1)}, f32[3,4,1024]{2,1,0:T(4,128)}, /*index=5*/f32[1,1024]{1,0:T(1,128)}) custom-call(bf16[512,1024]{1,0:T(8,128)(2,1)} %q_hbm.1, bf16[512,1024]{1,0:T(8,128)(2,1)} %k_hbm.1, bf16[512,1024]{1,0:T(8,128)(2,1)} %v_hbm.1, ...), custom_call_target="tpu_custom_call" | custom-call | tf_op jit(solution)/shard_map/pallas_call | solution.py:545
  65.8 5.3 %shard_map.119 = (bf16[512,1024]{1,0:T(8,128)(2,1)}, bf16[512,1024]{1,0:T(8,128)(2,1)}, bf16[512,1024]{1,0:T(8,128)(2,1)}, bf16[512,1024]{1,0:T(8,128)(2,1)}, f32[3,4,1024]{2,1,0:T(4,128)}, /*index=5*/f32[1,1024]{1,0:T(1,128)}) custom-call(bf16[512,1024]{1,0:T(8,128)(2,1)} %get-tuple-element.18.refs_0_, bf16[512,1024]{1,0:T(8,128)(2,1)} %get-tuple-element.19.refs_1_, ...), custom_call_target="tpu_custom_call" | custom-call | tf_op jit(solution)/shard_map/pallas_call | solution.py:606
